TPU v7x, 32 devices: a whole 2x2x4 slice. The times are simulated.
32 devices in a mesh: ctx: 8 (over y, x, core), ch: 4 (over z).
Axes of the slice: x: 2, y: 2, z: 4, core: 2. Of those that a mesh axis runs over, the one named last changes fastest.
Arguments:
- latent: bfloat16 [16, 256, 640], P('ctx', 'ch'), may hold values from -6 to 6
- cotangent: bfloat16 [32, 256, 640], P('ctx', 'ch'), may hold values from -6 to 6
- weight: bfloat16 [27, 256, 256], P(None, 'ch'), may hold values from -0.078125 to 0.078125
- clip_ids: int32 [16], replicated, may hold values from 0 to 3, never falling along the last dimension, each value on 1 to 6 neighbouring positions
Outputs:
- grad_latent: bfloat16 [16, 256, 640], P('ctx', 'ch')
- grad_weight: float32 [27, 256, 256], P(None, 'ch', 'ctx')
Inputs may be any that keep to these rules, and one draw needn't show every extreme that they name: `clip_ids`: clip ids never fall along the frames; each clip holds 1 to 6 frames and one holds exactly that many.
All inputs are finite; a program needn't handle non-finite values.
Results may differ from a plain program's by a relative error of at most 0.0049.
Values may be sent and summed in bfloat16 or wider, within the bound.
A program may use at most 128 MiB of HBM per device.

v0:
```python
import functools

import jax
import jax.numpy as jnp
from jax import lax
from jax.experimental import pallas as pl
from jax.experimental.pallas import tpu as pltpu
from jax.sharding import PartitionSpec as P

HB = 4
WW = 160
CELLS = HB * WW
MESH = pl.DeviceIdType.MESH

offsets = [(r_off, c_off) for r_off in (-1, 0, 1) for c_off in (-1, 0, 1)]


def edge_masks():
    cell = lax.broadcasted_iota(jnp.int32, (1, CELLS), 1)
    row, col = cell // WW, cell % WW
    masks = {}
    for r, c in offsets:
        inside = (row + r >= 0) & (row + r < HB) & (col + c >= 0) & (col + c < WW)
        masks[r, c] = inside.astype(jnp.float32)
    return masks


def moved(value, r, c, masks):
    step = r * WW + c
    if step == 0:
        return value
    return pltpu.roll(value, (-step) % CELLS, 1) * masks[r, c]


def kernel(
    n_ctx, n_ch, ids_ref, latent_ref, cot_ref, w_ref, gl_ref, gw_ref,
    xg, wt, terms, fwd_out, fwd_in, bwd_out, bwd_in, grads, stack, sx, rx, acc, sw, rw,
    gat_send, gat_recv, halo_send, halo_recv, x_send, x_recv, w_send, w_recv,
):
    ctx, ch = lax.axis_index("ctx"), lax.axis_index("ch")
    frames, own = latent_ref.shape[0], latent_ref.shape[1]
    rows = w_ref.shape[0] * own
    width = w_ref.shape[2]
    share = width // n_ctx
    f32, bf16 = jnp.float32, jnp.bfloat16

    for d in range(1, n_ch):
        pl.semaphore_signal(pltpu.get_barrier_semaphore(), inc=1,
                            device_id=(ctx, lax.rem(ch + d, n_ch)), device_id_type=MESH)
    for d in range(1, n_ctx):
        pl.semaphore_signal(pltpu.get_barrier_semaphore(), inc=1,
                            device_id=(lax.rem(ctx + d, n_ctx), ch), device_id_type=MESH)
    for s in range(frames):
        xg[s, ch] = latent_ref[s]
    pl.semaphore_wait(pltpu.get_barrier_semaphore(), n_ch + n_ctx - 2)

    def hop(way, step, s):
        chunk = ch - step if way == 0 else ch + step
        peer = ch + 1 if way == 0 else ch - 1
        return pltpu.make_async_remote_copy(
            src_ref=xg.at[s, chunk], dst_ref=xg.at[s, chunk],
            send_sem=gat_send.at[way, step, s], recv_sem=gat_recv.at[way, step, s],
            device_id=(ctx, peer), device_id_type=MESH)

    def landing(way, step, s):
        chunk = ch - 1 - step if way == 0 else ch + 1 + step
        peer = ch - 1 if way == 0 else ch + 1
        return pltpu.make_async_remote_copy(
            src_ref=xg.at[s, chunk], dst_ref=xg.at[s, chunk],
            send_sem=gat_send.at[way, step, s], recv_sem=gat_recv.at[way, step, s],
            device_id=(ctx, peer), device_id_type=MESH)

    def has(way, step):
        return ch - step >= 0 if way == 0 else ch + step < n_ch

    def sends(way, step):
        if way == 0:
            return (ch - step >= 0) & (ch + 1 < n_ch)
        return (ch + step < n_ch) & (ch >= 1)

    for step in range(n_ch):
        if step == 1:
            wt[...] = jnp.transpose(w_ref[...].reshape(rows, width))
        for s in reversed(range(frames)):
            for way in range(2):
                if step > 0:
                    @pl.when(has(way, step))
                    def _(way=way, step=step, s=s):
                        landing(way, step - 1, s).wait_recv()
                if step < n_ch - 1:
                    @pl.when(sends(way, step))
                    def _(way=way, step=step, s=s):
                        hop(way, step, s).start()

    masks = edge_masks()
    last = frames - 1

    def convolve(s):
        x = xg[s].reshape(width, CELLS)
        for k in range(3):
            prod = jnp.dot(w_ref[9 * k : 9 * k + 9].reshape(9 * own, width), x,
                           preferred_element_type=f32)
            total = None
            for spot, (r, c) in enumerate(offsets):
                part = moved(prod[spot * own : (spot + 1) * own], r, c, masks)
                total = part if total is None else total + part
            terms[s, k] = total

    def fwd_copy():
        return pltpu.make_async_remote_copy(
            src_ref=fwd_out, dst_ref=fwd_in, send_sem=halo_send.at[0], recv_sem=halo_recv.at[0],
            device_id=(lax.rem(ctx + 1, n_ctx), ch), device_id_type=MESH)

    def bwd_copy():
        return pltpu.make_async_remote_copy(
            src_ref=bwd_out, dst_ref=bwd_in, send_sem=halo_send.at[1], recv_sem=halo_recv.at[1],
            device_id=(lax.rem(ctx + n_ctx - 1, n_ctx), ch), device_id_type=MESH)

    convolve(last)
    fwd_out[0] = (terms[last, 1] + terms[last, 2]).astype(bf16)
    fwd_out[1] = terms[last, 2].astype(bf16)

    @pl.when(ctx + 1 < n_ctx)
    def _():
        fwd_copy().start()

    for s in reversed(range(last)):
        convolve(s)

    def same(a, b):
        return (ids_ref[a] == ids_ref[b]).astype(f32)

    base = ctx * frames
    top = n_ctx * frames - 1

    def joined(s):
        low = jnp.maximum(base + s - 1, 0) if s == 0 else base + s - 1
        return same(low, base + s)

    def slopes(s, both, late):
        gate = joined(s)
        for odd in range(2):
            if odd == 0:
                pre = terms[s, 0] + gate * both
            else:
                pre = terms[s, 0] + terms[s, 1] + gate * late
            sig = jax.nn.sigmoid(pre)
            slope = sig * (1.0 + pre * (1.0 - sig))
            grads[2 * s + odd] = (cot_ref[2 * s + odd].astype(f32) * slope).astype(bf16)

    for s in range(1, frames):
        slopes(s, terms[s - 1, 1] + terms[s - 1, 2], terms[s - 1, 2])

    @pl.when(ctx > 0)
    def _():
        fwd_copy().wait_recv()

    @pl.when(ctx == 0)
    def _():
        fwd_in[...] = jnp.zeros_like(fwd_in)

    slopes(0, fwd_in[0].astype(f32), fwd_in[1].astype(f32))
    bwd_out[0] = grads[0]
    bwd_out[1] = (grads[0].astype(f32) + grads[1].astype(f32)).astype(bf16)

    @pl.when(ctx > 0)
    def _():
        bwd_copy().start()

    def x_copy(s, d):
        peer = lax.rem(ch + d, n_ch)
        return pltpu.make_async_remote_copy(
            src_ref=sx.at[s, peer], dst_ref=rx.at[s, d],
            send_sem=x_send.at[s, d], recv_sem=x_recv.at[s, d],
            device_id=(ctx, peer), device_id_type=MESH)

    def w_copy(d):
        peer = lax.rem(ctx + d, n_ctx)
        return pltpu.make_async_remote_copy(
            src_ref=sw.at[peer], dst_ref=rw.at[d],
            send_sem=w_send.at[d], recv_sem=w_recv.at[d],
            device_id=(peer, ch), device_id_type=MESH)

    for s in range(frames):
        if s == last:
            @pl.when(ctx + 1 < n_ctx)
            def _():
                bwd_copy().wait_recv()

            @pl.when(ctx + 1 == n_ctx)
            def _():
                bwd_in[...] = jnp.zeros_like(bwd_in)

            after, pair = bwd_in[0].astype(f32), bwd_in[1].astype(f32)
            gate = same(base + s, jnp.minimum(base + s + 1, top))
        else:
            after = grads[2 * s + 2].astype(f32)
            pair = after + grads[2 * s + 3].astype(f32)
            gate = same(base + s, base + s + 1)
        odd = grads[2 * s + 1].astype(f32)
        groups = [grads[2 * s].astype(f32) + odd, odd + gate * after, gate * pair]
        for k in range(3):
            for spot, (r, c) in enumerate(offsets):
                tap = 9 * k + spot
                stack[s, tap * own : (tap + 1) * own] = moved(groups[k], -r, -c, masks).astype(bf16)
        dx = jnp.dot(wt[...], stack[s], preferred_element_type=f32)
        sx[s] = dx.reshape(n_ch, own, CELLS).astype(bf16)
        for d in range(1, n_ch):
            x_copy(s, d).start()
        x = xg[s].reshape(width, CELLS)
        dw = lax.dot_general(x, stack[s], (((1,), (1,)), ((), ())), preferred_element_type=f32)
        if s == 0:
            acc[...] = dw
        elif s < last:
            acc[...] += dw
        else:
            sw[...] = (acc[...] + dw if frames > 1 else dw).reshape(n_ctx, share, rows).astype(bf16)
    for d in range(1, n_ctx):
        w_copy(d).start()

    for s in range(frames):
        total = sx[s, ch].astype(f32)
        for d in range(1, n_ch):
            x_copy(s, d).wait_recv()
            total = total + rx[s, d].astype(f32)
        gl_ref[s] = total.astype(bf16)
    total = sw[ctx].astype(f32)
    for d in range(1, n_ctx):
        w_copy(d).wait_recv()
        total = total + rw[d].astype(f32)
    gw_ref[...] = jnp.transpose(total).reshape(gw_ref.shape)

    for step in range(n_ch - 1):
        for s in range(frames):
            for way in range(2):
                @pl.when(sends(way, step))
                def _(way=way, step=step, s=s):
                    hop(way, step, s).wait_send()

    @pl.when(ctx + 1 < n_ctx)
    def _():
        fwd_copy().wait_send()

    @pl.when(ctx > 0)
    def _():
        bwd_copy().wait_send()

    for s in range(frames):
        for d in range(1, n_ch):
            x_copy(s, d).wait_send()
    for d in range(1, n_ctx):
        w_copy(d).wait_send()


def on_device(n_ctx, n_ch, latent, cotangent, weight, clip_ids):
    frames, own = latent.shape[:2]
    taps, _, width = weight.shape
    rows, share = taps * own, width // n_ctx
    bf16, f32 = jnp.bfloat16, jnp.float32
    dma = pltpu.SemaphoreType.DMA
    vmem = pl.BlockSpec(memory_space=pltpu.VMEM)
    return pl.pallas_call(
        functools.partial(kernel, n_ctx, n_ch),
        out_shape=(
            jax.ShapeDtypeStruct(latent.shape, bf16),
            jax.ShapeDtypeStruct((taps, own, share), f32),
        ),
        in_specs=[pl.BlockSpec(memory_space=pltpu.SMEM), vmem, vmem, vmem],
        out_specs=(vmem, vmem),
        scratch_shapes=[
            pltpu.VMEM((frames, n_ch, own, CELLS), bf16),
            pltpu.VMEM((width, rows), bf16),
            pltpu.VMEM((frames, 3, own, CELLS), f32),
            pltpu.VMEM((2, own, CELLS), bf16),
            pltpu.VMEM((2, own, CELLS), bf16),
            pltpu.VMEM((2, own, CELLS), bf16),
            pltpu.VMEM((2, own, CELLS), bf16),
            pltpu.VMEM((2 * frames, own, CELLS), bf16),
            pltpu.VMEM((frames, rows, CELLS), bf16),
            pltpu.VMEM((frames, n_ch, own, CELLS), bf16),
            pltpu.VMEM((frames, n_ch, own, CELLS), bf16),
            pltpu.VMEM((width, rows), f32),
            pltpu.VMEM((n_ctx, share, rows), bf16),
            pltpu.VMEM((n_ctx, share, rows), bf16),
            dma((2, n_ch - 1, frames)),
            dma((2, n_ch - 1, frames)),
            dma((2,)),
            dma((2,)),
            dma((frames, n_ch)),
            dma((frames, n_ch)),
            dma((n_ctx,)),
            dma((n_ctx,)),
        ],
        compiler_params=pltpu.CompilerParams(
            collective_id=0, has_side_effects=True, vmem_limit_bytes=48 * 1024 * 1024
        ),
    )(clip_ids, latent, cotangent, weight)


def solution(mesh):
    placed = (P("ctx", "ch", None), P("ctx", "ch", None), P(None, "ch", None), P())
    return jax.shard_map(
        functools.partial(on_device, mesh.shape["ctx"], mesh.shape["ch"]),
        mesh=mesh,
        in_specs=placed,
        out_specs=(P("ctx", "ch", None), P(None, "ch", "ctx")),
        check_vma=False,
    )
```

profile of v0, /device:TPU:1, one launch (start us, length us, event | category | flops | bytes accessed | tf_op | source)
XLA Modules:
  0.0 47.8 jit_solution(542594461874920315)
XLA Ops:
  0.6 0.0 copy-start
  0.6 1.2 %copy-done = bf16[27,64,256]{2,1,0:T(8,128)(2,1)S(1)} copy-done((bf16[27,64,256]{2,1,0:T(8,128)(2,1)S(1)}, bf16[27,64,256]{2,1,0:T(8,128)(2,1)}, u32[]{:S(2)}) %copy-start) | copy-done | bytes 884760
  1.8 0.0 copy-start.1
  1.8 1.0 %copy-done.1 = bf16[4,64,640]{2,1,0:T(8,128)(2,1)S(1)} copy-done((bf16[4,64,640]{2,1,0:T(8,128)(2,1)S(1)}, bf16[4,64,640]{2,1,0:T(8,128)(2,1)}, u32[]{:S(2)}) %copy-start.1) | copy-done | bytes 327704
  2.8 0.0 copy-start.2
  2.8 0.9 %copy-done.2 = bf16[2,64,640]{2,1,0:T(8,128)(2,1)S(1)} copy-done((bf16[2,64,640]{2,1,0:T(8,128)(2,1)S(1)}, bf16[2,64,640]{2,1,0:T(8,128)(2,1)}, u32[]{:S(2)}) %copy-start.2) | copy-done | bytes 163864
  3.7 0.0 copy-start.3
  3.7 0.7 %copy-done.3 = s32[16]{0:T(128)S(1)} copy-done((s32[16]{0:T(128)S(1)}, s32[16]{0:T(128)}, u32[]{:S(2)}) %copy-start.3) | copy-done | bytes 88
  4.3 41.8 %shard_map.59 = (bf16[2,64,640]{2,1,0:T(8,128)(2,1)S(1)}, f32[27,64,32]{2,1,0:T(8,128)S(1)}) custom-call(s32[16]{0:T(128)S(1)} %copy-done.3, bf16[2,64,640]{2,1,0:T(8,128)(2,1)S(1)} %copy-done.2, bf16[4,64,640]{2,1,0:T(8,128)(2,1)S(1)} %copy-done.1, bf16[27,64,256]{2,1,0:T(8,128)(2,1)S(1)} %copy-done), custom_call_target="tpu_custom_call" | custom-call | tf_op jit(solution)/shard_map/pallas_call | solution.py:262
  46.1 1.1 %copy.6 = f32[27,64,32]{1,2,0:T(8,128)} copy(f32[27,64,32]{2,1,0:T(8,128)S(1)} %get-tuple-element.3) | data formatting | bytes 442368 | tf_op jit(solution)/shard_map/pallas_call | solution.py:262
  47.2 0.7 %copy.8 = bf16[2,64,640]{2,1,0:T(8,128)(2,1)} copy(bf16[2,64,640]{2,1,0:T(8,128)(2,1)S(1)} %get-tuple-element.6) | data formatting | bytes 327680
Async XLA Ops:
  0.6 1.2 %copy-start = (bf16[27,64,256]{2,1,0:T(8,128)(2,1)S(1)}, bf16[27,64,256]{2,1,0:T(8,128)(2,1)}, u32[]{:S(2)}) copy-start(bf16[27,64,256]{2,1,0:T(8,128)(2,1)} %w_ref.1) | copy-start | bytes 2654212
  1.8 1.0 %copy-start.1 = (bf16[4,64,640]{2,1,0:T(8,128)(2,1)S(1)}, bf16[4,64,640]{2,1,0:T(8,128)(2,1)}, u32[]{:S(2)}) copy-start(bf16[4,64,640]{2,1,0:T(8,128)(2,1)} %cot_ref.1) | copy-start | bytes 983044
  2.8 0.9 %copy-start.2 = (bf16[2,64,640]{2,1,0:T(8,128)(2,1)S(1)}, bf16[2,64,640]{2,1,0:T(8,128)(2,1)}, u32[]{:S(2)}) copy-start(bf16[2,64,640]{2,1,0:T(8,128)(2,1)} %latent_ref.1) | copy-start | bytes 491524
  3.7 0.7 %copy-start.3 = (s32[16]{0:T(128)S(1)}, s32[16]{0:T(128)}, u32[]{:S(2)}) copy-start(s32[16]{0:T(128)} %ids_ref.1) | copy-start | bytes 196
where the time goes:
time: 48.1 us; the launch traced here: 47.8 us
  Pallas kernels  41.8 us (87%)
  local copies, waits for them, and re-layouts  5.42 us (11%)
  between operations  0.65 us (1%)
    pallas_call x1, Pallas kernels, on_device(): pl.pallas_call(functools.partial(kernel, n_ctx, n_ch), out_shape=(jax.Sha...  41.8 us
    unnamed x9, local copies, waits for them, and re-layouts  4.37 us
    pallas_call x1, local copies, waits for them, and re-layouts, on_device(): pl.pallas_call(functools.partial(kernel, n_ctx, n_ch), out_shape=(jax.Sha...  1.06 us

commit v1 on v0

--- a/solution.py
+++ b/solution.py
@@ -33,25 +33,33 @@
 
 
 def kernel(
-    n_ctx, n_ch, ids_ref, latent_ref, cot_ref, w_ref, gl_ref, gw_ref,
-    xg, wt, terms, fwd_out, fwd_in, bwd_out, bwd_in, grads, stack, sx, rx, acc, sw, rw,
-    gat_send, gat_recv, halo_send, halo_recv, x_send, x_recv, w_send, w_recv,
+    n_ctx, n_ch, ids_ref, latent_hbm, cot_hbm, w_hbm, gl_ref, gw_ref,
+    w_ref, cot_ref, xg, wt, terms, fwd_out, fwd_in, bwd_out, bwd_in, grads, stack, sx, rx, acc, sw, rw,
+    load_sem, gat_send, gat_recv, halo_send, halo_recv, x_send, x_recv, w_send, w_recv,
 ):
     ctx, ch = lax.axis_index("ctx"), lax.axis_index("ch")
-    frames, own = latent_ref.shape[0], latent_ref.shape[1]
+    frames, own = latent_hbm.shape[0], latent_hbm.shape[1]
     rows = w_ref.shape[0] * own
     width = w_ref.shape[2]
     share = width // n_ctx
     f32, bf16 = jnp.float32, jnp.bfloat16
 
+    loads = [
+        pltpu.make_async_copy(latent_hbm.at[s], xg.at[s, ch], load_sem.at[s])
+        for s in range(frames)
+    ]
+    loads.append(pltpu.make_async_copy(w_hbm, w_ref, load_sem.at[frames]))
+    loads.append(pltpu.make_async_copy(cot_hbm, cot_ref, load_sem.at[frames + 1]))
+    for load in reversed(loads[:frames]):
+        load.start()
+    for load in loads[frames:]:
+        load.start()
     for d in range(1, n_ch):
         pl.semaphore_signal(pltpu.get_barrier_semaphore(), inc=1,
                             device_id=(ctx, lax.rem(ch + d, n_ch)), device_id_type=MESH)
     for d in range(1, n_ctx):
         pl.semaphore_signal(pltpu.get_barrier_semaphore(), inc=1,
                             device_id=(lax.rem(ctx + d, n_ctx), ch), device_id_type=MESH)
-    for s in range(frames):
-        xg[s, ch] = latent_ref[s]
     pl.semaphore_wait(pltpu.get_barrier_semaphore(), n_ch + n_ctx - 2)
 
     def hop(way, step, s):
@@ -78,19 +86,27 @@
             return (ch - step >= 0) & (ch + 1 < n_ch)
         return (ch + step < n_ch) & (ch >= 1)
 
-    for step in range(n_ch):
+    for step in range(n_ch - 1):
         if step == 1:
+            loads[frames].wait()
             wt[...] = jnp.transpose(w_ref[...].reshape(rows, width))
         for s in reversed(range(frames)):
+            if step == 0:
+                loads[s].wait()
             for way in range(2):
                 if step > 0:
                     @pl.when(has(way, step))
                     def _(way=way, step=step, s=s):
                         landing(way, step - 1, s).wait_recv()
-                if step < n_ch - 1:
-                    @pl.when(sends(way, step))
-                    def _(way=way, step=step, s=s):
-                        hop(way, step, s).start()
+                @pl.when(sends(way, step))
+                def _(way=way, step=step, s=s):
+                    hop(way, step, s).start()
+
+    def gathered(s):
+        for way in range(2):
+            @pl.when(has(way, n_ch - 1))
+            def _(way=way):
+                landing(way, n_ch - 2, s).wait_recv()
 
     masks = edge_masks()
     last = frames - 1
@@ -116,6 +132,7 @@
             src_ref=bwd_out, dst_ref=bwd_in, send_sem=halo_send.at[1], recv_sem=halo_recv.at[1],
             device_id=(lax.rem(ctx + n_ctx - 1, n_ctx), ch), device_id_type=MESH)
 
+    gathered(last)
     convolve(last)
     fwd_out[0] = (terms[last, 1] + terms[last, 2]).astype(bf16)
     fwd_out[1] = terms[last, 2].astype(bf16)
@@ -125,7 +142,9 @@
         fwd_copy().start()
 
     for s in reversed(range(last)):
+        gathered(s)
         convolve(s)
+    loads[frames + 1].wait()
 
     def same(a, b):
         return (ids_ref[a] == ids_ref[b]).astype(f32)
@@ -228,7 +247,8 @@
     for d in range(1, n_ctx):
         w_copy(d).wait_recv()
         total = total + rw[d].astype(f32)
-    gw_ref[...] = jnp.transpose(total).reshape(gw_ref.shape)
+    for tap in range(gw_ref.shape[0]):
+        gw_ref[tap] = total[:, tap * own : (tap + 1) * own]
 
     for step in range(n_ch - 1):
         for s in range(frames):
@@ -259,15 +279,18 @@
     bf16, f32 = jnp.bfloat16, jnp.float32
     dma = pltpu.SemaphoreType.DMA
     vmem = pl.BlockSpec(memory_space=pltpu.VMEM)
-    return pl.pallas_call(
+    hbm = pl.BlockSpec(memory_space=pltpu.HBM)
+    grad_latent, grad_weight = pl.pallas_call(
         functools.partial(kernel, n_ctx, n_ch),
         out_shape=(
             jax.ShapeDtypeStruct(latent.shape, bf16),
-            jax.ShapeDtypeStruct((taps, own, share), f32),
+            jax.ShapeDtypeStruct((taps, share, own), f32),
         ),
-        in_specs=[pl.BlockSpec(memory_space=pltpu.SMEM), vmem, vmem, vmem],
+        in_specs=[pl.BlockSpec(memory_space=pltpu.SMEM), hbm, hbm, hbm],
         out_specs=(vmem, vmem),
         scratch_shapes=[
+            pltpu.VMEM(weight.shape, bf16),
+            pltpu.VMEM(cotangent.shape, bf16),
             pltpu.VMEM((frames, n_ch, own, CELLS), bf16),
             pltpu.VMEM((width, rows), bf16),
             pltpu.VMEM((frames, 3, own, CELLS), f32),
@@ -282,6 +305,7 @@
             pltpu.VMEM((width, rows), f32),
             pltpu.VMEM((n_ctx, share, rows), bf16),
             pltpu.VMEM((n_ctx, share, rows), bf16),
+            dma((frames + 2,)),
             dma((2, n_ch - 1, frames)),
             dma((2, n_ch - 1, frames)),
             dma((2,)),
@@ -292,9 +316,10 @@
             dma((n_ctx,)),
         ],
         compiler_params=pltpu.CompilerParams(
-            collective_id=0, has_side_effects=True, vmem_limit_bytes=48 * 1024 * 1024
+            collective_id=0, has_side_effects=True, vmem_limit_bytes=64000 * 1024
         ),
     )(clip_ids, latent, cotangent, weight)
+    return grad_latent, jnp.swapaxes(grad_weight, 1, 2)
 
 
 def solution(mesh):

time: 48.1 us -> 44.2 us (0.919)
  local copies, waits for them, and re-layouts: 5.42 us -> 3.4 us
  Pallas kernels: 41.8 us -> 39.9 us
    pallas_call x1, Pallas kernels: 41.8 us -> 39.9 us  [on_device(): pl.pallas_call(functools.partial(kernel, n_ctx, n_ch), out_shape=(jax.Sha...]
    pallas_call x1 -> x0, local copies, waits for them, and re-layouts: 1.06 us -> none  [on_device(): pl.pallas_call(functools.partial(kernel, n_ctx, n_ch), out_shape=(jax.Sha...]
    unnamed x9 -> x2, local copies, waits for them, and re-layouts: 4.37 us -> 3.4 us
where the time goes in v1:
time: 44.2 us; the launch traced here: 44 us
  Pallas kernels  39.9 us (90%)
  local copies, waits for them, and re-layouts  3.4 us (8%)
  between operations  0.64 us (1%)
    pallas_call x1, Pallas kernels, on_device(): pl.pallas_call(functools.partial(kernel, n_ctx, n_ch), out_shape=(jax.Sha...  39.9 us
    unnamed x2, local copies, waits for them, and re-layouts  3.4 us

profile of v1, /device:TPU:1, one launch (start us, length us, event | category | flops | bytes accessed | tf_op | source)
XLA Modules:
  0.0 44.0 jit_solution(13829733527660727794)
XLA Ops:
  0.6 39.9 %shard_map.59 = (bf16[2,64,640]{2,1,0:T(8,128)(2,1)}, f32[27,32,64]{2,1,0:T(8,128)}) custom-call(s32[16]{0:T(128)} %ids_ref.1, bf16[2,64,640]{2,1,0:T(8,128)(2,1)} %latent_hbm.1, bf16[4,64,640]{2,1,0:T(8,128)(2,1)} %cot_hbm.1, bf16[27,64,256]{2,1,0:T(8,128)(2,1)} %w_hbm.1), custom_call_target="tpu_custom_call" | custom-call | tf_op jit(solution)/shard_map/pallas_call | solution.py:283
  40.6 1.6 %copy.8 = bf16[2,64,640]{2,1,0:T(8,128)(2,1)} copy(bf16[2,64,640]{2,1,0:T(8,128)(2,1)} %get-tuple-element.8) | data formatting | bytes 327680
  42.2 1.8 %copy.9 = f32[27,64,32]{1,2,0:T(8,128)} copy(f32[27,64,32]{1,2,0:T(8,128)} %bitcast.1) | data formatting | bytes 442368

commit v2 on v1

--- a/solution.py
+++ b/solution.py
@@ -62,54 +62,57 @@
                             device_id=(lax.rem(ctx + d, n_ctx), ch), device_id_type=MESH)
     pl.semaphore_wait(pltpu.get_barrier_semaphore(), n_ch + n_ctx - 2)
 
-    def hop(way, step, s):
-        chunk = ch - step if way == 0 else ch + step
-        peer = ch + 1 if way == 0 else ch - 1
+    ways = ((0, 1), (1, -1))
+    last = frames - 1
+
+    def inside(place):
+        return (place >= 0) & (place < n_ch)
+
+    def hop(way, sign, d, s):
+        chunk = ch - sign if d == 2 else ch
         return pltpu.make_async_remote_copy(
             src_ref=xg.at[s, chunk], dst_ref=xg.at[s, chunk],
-            send_sem=gat_send.at[way, step, s], recv_sem=gat_recv.at[way, step, s],
-            device_id=(ctx, peer), device_id_type=MESH)
-
-    def landing(way, step, s):
-        chunk = ch - 1 - step if way == 0 else ch + 1 + step
-        peer = ch - 1 if way == 0 else ch + 1
+            send_sem=gat_send.at[way, d - 1, s], recv_sem=gat_recv.at[way, d - 1, s],
+            device_id=(ctx, ch + sign if d == 2 else ch + sign * d), device_id_type=MESH)
+
+    def landing(way, sign, d, s):
+        chunk = ch - sign * d
         return pltpu.make_async_remote_copy(
             src_ref=xg.at[s, chunk], dst_ref=xg.at[s, chunk],
-            send_sem=gat_send.at[way, step, s], recv_sem=gat_recv.at[way, step, s],
-            device_id=(ctx, peer), device_id_type=MESH)
-
-    def has(way, step):
-        return ch - step >= 0 if way == 0 else ch + step < n_ch
-
-    def sends(way, step):
-        if way == 0:
-            return (ch - step >= 0) & (ch + 1 < n_ch)
-        return (ch + step < n_ch) & (ch >= 1)
-
-    for step in range(n_ch - 1):
-        if step == 1:
-            loads[frames].wait()
-            wt[...] = jnp.transpose(w_ref[...].reshape(rows, width))
-        for s in reversed(range(frames)):
-            if step == 0:
-                loads[s].wait()
-            for way in range(2):
-                if step > 0:
-                    @pl.when(has(way, step))
-                    def _(way=way, step=step, s=s):
-                        landing(way, step - 1, s).wait_recv()
-                @pl.when(sends(way, step))
-                def _(way=way, step=step, s=s):
-                    hop(way, step, s).start()
+            send_sem=gat_send.at[way, d - 1, s], recv_sem=gat_recv.at[way, d - 1, s],
+            device_id=(ctx, ch - sign), device_id_type=MESH)
+
+    def hops(sign, d):
+        return inside(ch - sign) & inside(ch + sign) if d == 2 else inside(ch + sign * d)
+
+    direct = [1] + list(range(3, n_ch))
+    for s in reversed(range(frames)):
+        loads[s].wait()
+        for d in direct:
+            for way, sign in ways:
+                @pl.when(hops(sign, d))
+                def _(way=way, sign=sign, d=d, s=s):
+                    hop(way, sign, d, s).start()
+    loads[frames].wait()
+    wt[...] = jnp.transpose(w_ref[...].reshape(rows, width))
+    for s in reversed(range(frames)):
+        for way, sign in ways:
+            @pl.when(inside(ch - sign))
+            def _(way=way, sign=sign, s=s):
+                landing(way, sign, 1, s).wait_recv()
+
+            @pl.when(hops(sign, 2))
+            def _(way=way, sign=sign, s=s):
+                hop(way, sign, 2, s).start()
 
     def gathered(s):
-        for way in range(2):
-            @pl.when(has(way, n_ch - 1))
-            def _(way=way):
-                landing(way, n_ch - 2, s).wait_recv()
+        for d in range(2, n_ch):
+            for way, sign in ways:
+                @pl.when(inside(ch - sign * d))
+                def _(way=way, sign=sign, d=d):
+                    landing(way, sign, d, s).wait_recv()
 
     masks = edge_masks()
-    last = frames - 1
 
     def convolve(s):
         x = xg[s].reshape(width, CELLS)
@@ -186,12 +189,36 @@
     def _():
         bwd_copy().start()
 
-    def x_copy(s, d):
-        peer = lax.rem(ch + d, n_ch)
-        return pltpu.make_async_remote_copy(
-            src_ref=sx.at[s, peer], dst_ref=rx.at[s, d],
-            send_sem=x_send.at[s, d], recv_sem=x_recv.at[s, d],
-            device_id=(ctx, peer), device_id_type=MESH)
+    def x_copy(way, sign, d, s):
+        return pltpu.make_async_remote_copy(
+            src_ref=sx.at[s, ch + sign * d], dst_ref=rx.at[s, way, d - 1],
+            send_sem=x_send.at[s, way, d - 1], recv_sem=x_recv.at[s, way, d - 1],
+            device_id=(ctx, ch + sign if d == 2 else ch + sign * d), device_id_type=MESH)
+
+    def x_landing(way, sign, d, s):
+        return pltpu.make_async_remote_copy(
+            src_ref=rx.at[s, way, d - 1], dst_ref=rx.at[s, way, d - 1],
+            send_sem=x_send.at[s, way, d - 1], recv_sem=x_recv.at[s, way, d - 1],
+            device_id=(ctx, ch - sign), device_id_type=MESH)
+
+    def x_start(s):
+        for d in range(2, n_ch):
+            for way, sign in ways:
+                @pl.when(inside(ch + sign * d))
+                def _(way=way, sign=sign, d=d):
+                    x_copy(way, sign, d, s).start()
+
+    def x_relay(s):
+        for way, sign in ways:
+            @pl.when(hops(sign, 2))
+            def _(way=way, sign=sign):
+                x_landing(way, sign, 2, s).wait_recv()
+                both = sx[s, ch + sign].astype(f32) + rx[s, way, 1].astype(f32)
+                sx[s, ch + sign] = both.astype(bf16)
+
+            @pl.when(inside(ch + sign))
+            def _(way=way, sign=sign):
+                x_copy(way, sign, 1, s).start()
 
     def w_copy(d):
         peer = lax.rem(ctx + d, n_ctx)
@@ -224,8 +251,9 @@
                 stack[s, tap * own : (tap + 1) * own] = moved(groups[k], -r, -c, masks).astype(bf16)
         dx = jnp.dot(wt[...], stack[s], preferred_element_type=f32)
         sx[s] = dx.reshape(n_ch, own, CELLS).astype(bf16)
-        for d in range(1, n_ch):
-            x_copy(s, d).start()
+        x_start(s)
+        if s > 0:
+            x_relay(s - 1)
         x = xg[s].reshape(width, CELLS)
         dw = lax.dot_general(x, stack[s], (((1,), (1,)), ((), ())), preferred_element_type=f32)
         if s == 0:
@@ -236,13 +264,18 @@
             sw[...] = (acc[...] + dw if frames > 1 else dw).reshape(n_ctx, share, rows).astype(bf16)
     for d in range(1, n_ctx):
         w_copy(d).start()
+    x_relay(last)
 
     for s in range(frames):
-        total = sx[s, ch].astype(f32)
-        for d in range(1, n_ch):
-            x_copy(s, d).wait_recv()
-            total = total + rx[s, d].astype(f32)
-        gl_ref[s] = total.astype(bf16)
+        terms[s, 0] = sx[s, ch].astype(f32)
+        for d in reversed(direct):
+            for way, sign in ways:
+                @pl.when(inside(ch - sign * d))
+                def _(way=way, sign=sign, d=d, s=s):
+                    x_landing(way, sign, d, s).wait_recv()
+                    terms[s, 0] += rx[s, way, d - 1].astype(f32)
+
+        gl_ref[s] = terms[s, 0].astype(bf16)
     total = sw[ctx].astype(f32)
     for d in range(1, n_ctx):
         w_copy(d).wait_recv()
@@ -250,24 +283,25 @@
     for tap in range(gw_ref.shape[0]):
         gw_ref[tap] = total[:, tap * own : (tap + 1) * own]
 
-    for step in range(n_ch - 1):
-        for s in range(frames):
-            for way in range(2):
-                @pl.when(sends(way, step))
-                def _(way=way, step=step, s=s):
-                    hop(way, step, s).wait_send()
-
-    @pl.when(ctx + 1 < n_ctx)
-    def _():
-        fwd_copy().wait_send()
-
-    @pl.when(ctx > 0)
-    def _():
-        bwd_copy().wait_send()
-
     for s in range(frames):
         for d in range(1, n_ch):
-            x_copy(s, d).wait_send()
+            for way, sign in ways:
+                @pl.when(hops(sign, d))
+                def _(way=way, sign=sign, d=d, s=s):
+                    hop(way, sign, d, s).wait_send()
+
+                @pl.when(inside(ch + sign * d))
+                def _(way=way, sign=sign, d=d, s=s):
+                    x_copy(way, sign, d, s).wait_send()
+
+    @pl.when(ctx + 1 < n_ctx)
+    def _():
+        fwd_copy().wait_send()
+
+    @pl.when(ctx > 0)
+    def _():
+        bwd_copy().wait_send()
+
     for d in range(1, n_ctx):
         w_copy(d).wait_send()
 
@@ -301,7 +335,7 @@
             pltpu.VMEM((2 * frames, own, CELLS), bf16),
             pltpu.VMEM((frames, rows, CELLS), bf16),
             pltpu.VMEM((frames, n_ch, own, CELLS), bf16),
-            pltpu.VMEM((frames, n_ch, own, CELLS), bf16),
+            pltpu.VMEM((frames, 2, n_ch - 1, own, CELLS), bf16),
             pltpu.VMEM((width, rows), f32),
             pltpu.VMEM((n_ctx, share, rows), bf16),
             pltpu.VMEM((n_ctx, share, rows), bf16),
@@ -310,8 +344,8 @@
             dma((2, n_ch - 1, frames)),
             dma((2,)),
             dma((2,)),
-            dma((frames, n_ch)),
-            dma((frames, n_ch)),
+            dma((frames, 2, n_ch - 1)),
+            dma((frames, 2, n_ch - 1)),
             dma((n_ctx,)),
             dma((n_ctx,)),
         ],

time: 44.2 us -> 43.2 us (0.977)
  the two profiles are of different devices: /device:TPU:1 before, /device:TPU:9 now
where the time goes in v2:
time: 43.2 us; the launch traced here: 43 us
  Pallas kernels  38.9 us (90%)
  local copies, waits for them, and re-layouts  3.4 us (8%)
  between operations  0.64 us (1%)
    pallas_call x1, Pallas kernels, on_device(): pl.pallas_call(functools.partial(kernel, n_ctx, n_ch), out_shape=(jax.Sha...  38.9 us
    unnamed x2, local copies, waits for them, and re-layouts  3.4 us

profile of v2, /device:TPU:9, one launch (start us, length us, event | category | flops | bytes accessed | tf_op | source)
XLA Modules:
  0.0 43.0 jit_solution(14426830860257274263)
XLA Ops:
  0.6 38.9 %shard_map.59 = (bf16[2,64,640]{2,1,0:T(8,128)(2,1)}, f32[27,32,64]{2,1,0:T(8,128)}) custom-call(s32[16]{0:T(128)} %ids_ref.1, bf16[2,64,640]{2,1,0:T(8,128)(2,1)} %latent_hbm.1, bf16[4,64,640]{2,1,0:T(8,128)(2,1)} %cot_hbm.1, bf16[27,64,256]{2,1,0:T(8,128)(2,1)} %w_hbm.1), custom_call_target="tpu_custom_call" | custom-call | tf_op jit(solution)/shard_map/pallas_call | solution.py:317
  39.6 1.6 %copy.8 = bf16[2,64,640]{2,1,0:T(8,128)(2,1)} copy(bf16[2,64,640]{2,1,0:T(8,128)(2,1)} %get-tuple-element.8) | data formatting | bytes 327680
  41.2 1.8 %copy.9 = f32[27,64,32]{1,2,0:T(8,128)} copy(f32[27,64,32]{1,2,0:T(8,128)} %bitcast.1) | data formatting | bytes 442368

commit v3 on v2

--- a/solution.py
+++ b/solution.py
@@ -34,8 +34,8 @@
 
 def kernel(
     n_ctx, n_ch, ids_ref, latent_hbm, cot_hbm, w_hbm, gl_ref, gw_ref,
-    w_ref, cot_ref, xg, wt, terms, fwd_out, fwd_in, bwd_out, bwd_in, grads, stack, sx, rx, acc, sw, rw,
-    load_sem, gat_send, gat_recv, halo_send, halo_recv, x_send, x_recv, w_send, w_recv,
+    w_ref, cot_ref, xg, wt, terms, fwd_out, fwd_in, bwd_out, bwd_in, grads, stack, sx, rx, acc, sw, rc, rw,
+    load_sem, gat_send, gat_recv, halo_send, halo_recv, x_send, x_recv, c_send, c_recv, w_send, w_recv,
 ):
     ctx, ch = lax.axis_index("ctx"), lax.axis_index("ch")
     frames, own = latent_hbm.shape[0], latent_hbm.shape[1]
@@ -220,12 +220,21 @@
             def _(way=way, sign=sign):
                 x_copy(way, sign, 1, s).start()
 
+    half = n_ctx // 2
+    side, pair_at = lax.rem(ctx, 2), ctx // 2
+
+    def core_copy(q):
+        return pltpu.make_async_remote_copy(
+            src_ref=sw.at[1 - side, q], dst_ref=rc.at[q],
+            send_sem=c_send.at[q], recv_sem=c_recv.at[q],
+            device_id=(ctx + 1 - 2 * side, ch), device_id_type=MESH)
+
     def w_copy(d):
-        peer = lax.rem(ctx + d, n_ctx)
-        return pltpu.make_async_remote_copy(
-            src_ref=sw.at[peer], dst_ref=rw.at[d],
+        q = lax.rem(pair_at + d, half)
+        return pltpu.make_async_remote_copy(
+            src_ref=sw.at[side, q], dst_ref=rw.at[d],
             send_sem=w_send.at[d], recv_sem=w_recv.at[d],
-            device_id=(peer, ch), device_id_type=MESH)
+            device_id=(2 * q + side, ch), device_id_type=MESH)
 
     for s in range(frames):
         if s == last:
@@ -261,10 +270,17 @@
         elif s < last:
             acc[...] += dw
         else:
-            sw[...] = (acc[...] + dw if frames > 1 else dw).reshape(n_ctx, share, rows).astype(bf16)
-    for d in range(1, n_ctx):
+            full = (acc[...] + dw if frames > 1 else dw).reshape(half, 2, share, rows)
+            for p in range(2):
+                sw[p] = full[:, p].astype(bf16)
+    for q in range(half):
+        core_copy(q).start()
+    x_relay(last)
+    for q in range(half):
+        core_copy(q).wait_recv()
+        sw[side, q] = (sw[side, q].astype(f32) + rc[q].astype(f32)).astype(bf16)
+    for d in range(1, half):
         w_copy(d).start()
-    x_relay(last)
 
     for s in range(frames):
         terms[s, 0] = sx[s, ch].astype(f32)
@@ -276,8 +292,8 @@
                     terms[s, 0] += rx[s, way, d - 1].astype(f32)
 
         gl_ref[s] = terms[s, 0].astype(bf16)
-    total = sw[ctx].astype(f32)
-    for d in range(1, n_ctx):
+    total = sw[side, pair_at].astype(f32)
+    for d in range(1, half):
         w_copy(d).wait_recv()
         total = total + rw[d].astype(f32)
     for tap in range(gw_ref.shape[0]):
@@ -302,7 +318,9 @@
     def _():
         bwd_copy().wait_send()
 
-    for d in range(1, n_ctx):
+    for q in range(half):
+        core_copy(q).wait_send()
+    for d in range(1, half):
         w_copy(d).wait_send()
 
 
@@ -337,8 +355,9 @@
             pltpu.VMEM((frames, n_ch, own, CELLS), bf16),
             pltpu.VMEM((frames, 2, n_ch - 1, own, CELLS), bf16),
             pltpu.VMEM((width, rows), f32),
-            pltpu.VMEM((n_ctx, share, rows), bf16),
-            pltpu.VMEM((n_ctx, share, rows), bf16),
+            pltpu.VMEM((2, n_ctx // 2, share, rows), bf16),
+            pltpu.VMEM((n_ctx // 2, share, rows), bf16),
+            pltpu.VMEM((n_ctx // 2, share, rows), bf16),
             dma((frames + 2,)),
             dma((2, n_ch - 1, frames)),
             dma((2, n_ch - 1, frames)),
@@ -346,8 +365,10 @@
             dma((2,)),
             dma((frames, 2, n_ch - 1)),
             dma((frames, 2, n_ch - 1)),
-            dma((n_ctx,)),
-            dma((n_ctx,)),
+            dma((n_ctx // 2,)),
+            dma((n_ctx // 2,)),
+            dma((n_ctx // 2,)),
+            dma((n_ctx // 2,)),
         ],
         compiler_params=pltpu.CompilerParams(
             collective_id=0, has_side_effects=True, vmem_limit_bytes=64000 * 1024

time: 43.2 us -> 41.8 us (0.968)
  the two profiles are of different devices: /device:TPU:9 before, /device:TPU:17 now
where the time goes in v3:
time: 41.8 us; the launch traced here: 41.7 us
  Pallas kernels  37.6 us (90%)
  local copies, waits for them, and re-layouts  3.4 us (8%)
  between operations  0.64 us (2%)
    pallas_call x1, Pallas kernels, on_device(): pl.pallas_call(functools.partial(kernel, n_ctx, n_ch), out_shape=(jax.Sha...  37.6 us
    unnamed x2, local copies, waits for them, and re-layouts  3.4 us

profile of v3, /device:TPU:17, one launch (start us, length us, event | category | flops | bytes accessed | tf_op | source)
XLA Modules:
  0.0 41.7 jit_solution(17282329297902693799)
XLA Ops:
  0.6 37.6 %shard_map.59 = (bf16[2,64,640]{2,1,0:T(8,128)(2,1)}, f32[27,32,64]{2,1,0:T(8,128)}) custom-call(s32[16]{0:T(128)} %ids_ref.1, bf16[2,64,640]{2,1,0:T(8,128)(2,1)} %latent_hbm.1, bf16[4,64,640]{2,1,0:T(8,128)(2,1)} %cot_hbm.1, bf16[27,64,256]{2,1,0:T(8,128)(2,1)} %w_hbm.1), custom_call_target="tpu_custom_call" | custom-call | tf_op jit(solution)/shard_map/pallas_call | solution.py:335
  38.3 1.6 %copy.8 = bf16[2,64,640]{2,1,0:T(8,128)(2,1)} copy(bf16[2,64,640]{2,1,0:T(8,128)(2,1)} %get-tuple-element.8) | data formatting | bytes 327680
  39.8 1.8 %copy.9 = f32[27,64,32]{1,2,0:T(8,128)} copy(f32[27,64,32]{1,2,0:T(8,128)} %bitcast.1) | data formatting | bytes 442368

commit v4 on v3

--- a/solution.py
+++ b/solution.py
@@ -275,12 +275,12 @@
                 sw[p] = full[:, p].astype(bf16)
     for q in range(half):
         core_copy(q).start()
-    x_relay(last)
     for q in range(half):
         core_copy(q).wait_recv()
         sw[side, q] = (sw[side, q].astype(f32) + rc[q].astype(f32)).astype(bf16)
     for d in range(1, half):
         w_copy(d).start()
+    x_relay(last)
 
     for s in range(frames):
         terms[s, 0] = sx[s, ch].astype(f32)

time: 41.8 us -> 39.9 us (0.955)
  the two profiles are of different devices: /device:TPU:17 before, /device:TPU:1 now
where the time goes in v4:
time: 39.9 us; the launch traced here: 39.4 us
  Pallas kernels  35.4 us (89%)
  local copies, waits for them, and re-layouts  3.4 us (9%)
  between operations  0.64 us (2%)
    pallas_call x1, Pallas kernels, on_device(): pl.pallas_call(functools.partial(kernel, n_ctx, n_ch), out_shape=(jax.Sha...  35.4 us
    unnamed x2, local copies, waits for them, and re-layouts  3.4 us

profile of v4, /device:TPU:1, one launch (start us, length us, event | category | flops | bytes accessed | tf_op | source)
XLA Modules:
  0.0 39.4 jit_solution(14978421110109019763)
XLA Ops:
  0.6 35.4 %shard_map.59 = (bf16[2,64,640]{2,1,0:T(8,128)(2,1)}, f32[27,32,64]{2,1,0:T(8,128)}) custom-call(s32[16]{0:T(128)} %ids_ref.1, bf16[2,64,640]{2,1,0:T(8,128)(2,1)} %latent_hbm.1, bf16[4,64,640]{2,1,0:T(8,128)(2,1)} %cot_hbm.1, bf16[27,64,256]{2,1,0:T(8,128)(2,1)} %w_hbm.1), custom_call_target="tpu_custom_call" | custom-call | tf_op jit(solution)/shard_map/pallas_call | solution.py:335
  36.0 1.6 %copy.8 = bf16[2,64,640]{2,1,0:T(8,128)(2,1)} copy(bf16[2,64,640]{2,1,0:T(8,128)(2,1)} %get-tuple-element.8) | data formatting | bytes 327680
  37.6 1.8 %copy.9 = f32[27,64,32]{1,2,0:T(8,128)} copy(f32[27,64,32]{1,2,0:T(8,128)} %bitcast.1) | data formatting | bytes 442368
